TPU v7x, 128 devices: a whole 4x4x4 slice. The times are simulated.
128 devices in a mesh: ctx: 32 (over y_hi, x, z), fsdp: 4 (over y_lo, core).
Axes of the slice: x: 4, y: 4 (y_hi: 2, y_lo: 2; y = y_hi * 2 + y_lo), z: 4, core: 2. Of those that a mesh axis runs over, the one named last changes fastest.
Arguments:
- layer_input: bfloat16 [4, 4096, 1024], P('fsdp', 'ctx'), may hold values from -6 to 6
- cotangent: bfloat16 [4, 4096, 1024], P('fsdp', 'ctx'), may hold values from -6 to 6
- block_order: int32 [4, 64], P('fsdp'), may hold values from 0 to 63, as said below
- query_weight: bfloat16 [1024, 2048], P('fsdp'), may hold values from -0.1875 to 0.1875
- key_projection: bfloat16 [1024, 1024], P('fsdp'), may hold values from -0.1875 to 0.1875
- value_projection: bfloat16 [1024, 1024], P('fsdp'), may hold values from -0.1875 to 0.1875
- output_weight: bfloat16 [2048, 1024], P('fsdp'), may hold values from -0.75 to 0.75
- gate_weight: bfloat16 [1024, 3072], P('fsdp'), may hold values from -0.1875 to 0.1875
- up_weight: bfloat16 [1024, 3072], P('fsdp'), may hold values from -0.1875 to 0.1875
- down_weight: bfloat16 [3072, 1024], P('fsdp'), may hold values from -0.109375 to 0.109375
- first_gain: float32 [1024], replicated, may hold values from 0.5 to 1.5
- second_gain: float32 [1024], replicated, may hold values from 0.5 to 1.5
- query_gain: float32 [128], replicated, may hold values from 0.25 to 1.75
- key_norm_gain: float32 [128], replicated, may hold values from 0.25 to 1.75
Outputs:
- layer_output: bfloat16 [4, 4096, 1024], P('fsdp', 'ctx')
- input_gradient: float32 [4, 4096, 1024], P('fsdp', 'ctx')
- query_weight_gradient: float32 [1024, 2048], P('fsdp')
- key_weight_gradient: float32 [1024, 1024], P('fsdp')
- value_weight_gradient: float32 [1024, 1024], P('fsdp')
- output_weight_gradient: float32 [2048, 1024], P('fsdp')
- gate_weight_gradient: float32 [1024, 3072], P('fsdp')
- up_weight_gradient: float32 [1024, 3072], P('fsdp')
- down_weight_gradient: float32 [3072, 1024], P('fsdp')
- first_gain_gradient: float32 [1024], P('fsdp')
- second_gain_gradient: float32 [1024], P('fsdp')
- query_gain_gradient: float32 [128], P('fsdp')
- key_gain_gradient: float32 [128], P('fsdp')
Inputs may be any that keep to these rules, and one draw needn't show every extreme that they name: Each row of block_order names every block of 64 positions of its sequence exactly once; the two blocks of rows 2 c and 2 c + 1 are mirrored, block b together with block 2 * 32 - 1 - b, in either order.
All inputs are finite; a program needn't handle non-finite values.
Results may differ from a plain program's by a relative error of at most 0.034.
Values may be sent and summed in bfloat16 or wider, within the bound.
No kernel may reach another device: no remote copies, remote signals or barrier semaphores. Data moves between devices by JAX's collectives and lax.ppermute only.
A program may use at most 320 MiB of HBM per device.

v0:
```python
import math
import jax
import jax.numpy as jnp
from jax import lax
from jax.sharding import PartitionSpec as P

HQ = 16
KEY_VALUE_HEADS = 8
HEAD_SIZE = 128
CTX = ("yh", "x", "z")
FSDP = ("yl", "c")
EPSILON = 1e-06
THETA = 1000000.0
MASKED = -1e30


def rms_apply(values, norm_gain):
    row_scale = lax.rsqrt(jnp.mean(values * values, axis=-1, keepdims=True) + EPSILON)
    normed = values * row_scale
    return (normed * norm_gain, normed, row_scale)


def root_mean_square_backward(gradient, normed, row_scale, norm_gain):
    normed_grad = gradient * norm_gain
    return row_scale * (
        normed_grad - normed * jnp.mean(normed_grad * normed, axis=-1, keepdims=True)
    )


def rope_tables(positions, head_width):
    half_width = head_width // 2
    inverse_freq = jnp.power(THETA, -2.0 * jnp.arange(half_width, dtype=jnp.float32) / head_width)
    angles = positions.astype(jnp.float32)[:, None] * inverse_freq[None, :]
    return (jnp.cos(angles)[:, None, :], jnp.sin(angles)[:, None, :])


def rotary_apply(values, cosine_table, sine_values_table):
    half_width = values.shape[-1] // 2
    front_half = values[..., :half_width]
    back_half = values[..., half_width:]
    return jnp.concatenate(
        [
            front_half * cosine_table - back_half * sine_values_table,
            back_half * cosine_table + front_half * sine_values_table,
        ],
        axis=-1,
    )


def rotary_backward(gradient, cosine_table, sine_values_table):
    half_width = gradient.shape[-1] // 2
    front_half = gradient[..., :half_width]
    back_half = gradient[..., half_width:]
    return jnp.concatenate(
        [
            front_half * cosine_table + back_half * sine_values_table,
            back_half * cosine_table - front_half * sine_values_table,
        ],
        axis=-1,
    )


def left_dot(left_side, right_side):
    return lax.dot_general(
        left_side, right_side, (((0,), (0,)), ((), ())), preferred_element_type=jnp.float32
    )


def right_dot(left_side, right_side):
    return lax.dot_general(
        left_side, right_side, (((1,), (1,)), ((), ())), preferred_element_type=jnp.float32
    )


def gather_fsdp(values):
    across = lax.all_gather(values, "yl", axis=0, tiled=False)
    both = lax.all_gather(across, "c", axis=1, tiled=False)
    return both.reshape((-1,) + values.shape[1:])


def reduce_ctx(shards):
    flat = jnp.concatenate([s.astype(jnp.bfloat16).reshape(-1) for s in shards])
    lanes = 128
    step = 256 * lanes
    padded = -(-flat.shape[0] // step) * step
    flat = jnp.pad(flat, (0, padded - flat.shape[0])).reshape(padded // lanes, lanes)
    part = lax.psum_scatter(flat, "z", scatter_dimension=0, tiled=True)
    part = lax.psum_scatter(part, "x", scatter_dimension=0, tiled=True)
    part = lax.psum(part, "yh")
    part = lax.all_gather(part, "x", axis=0, tiled=True)
    full = lax.all_gather(part, "z", axis=0, tiled=True).reshape(-1)
    out = []
    at = 0
    for s in shards:
        out.append(full[at : at + s.size].reshape(s.shape).astype(jnp.float32))
        at += s.size
    return tuple(out)


def on_device(
    layer_input,
    cotangent,
    block_order,
    query_weight,
    key_projection,
    value_projection,
    output_weight,
    gate_weight,
    up_weight,
    down_weight,
    first_gain,
    second_gain,
    query_gain,
    key_norm_gain,
):
    local_rows = layer_input.shape[1]
    block_rows = local_rows // 2
    ctx_size = lax.axis_size(CTX)
    halves = ctx_size // HQ
    half_devices = ctx_size // halves
    order_row = block_order[0]
    device_place = lax.axis_index(CTX)
    my_half = device_place // half_devices
    all_positions = (
        order_row[:, None] * block_rows + jnp.arange(block_rows, dtype=jnp.int32)[None, :]
    ).reshape(-1)
    own_positions = lax.dynamic_slice_in_dim(all_positions, device_place * local_rows, local_rows)
    cosine_table, sine_values_table = rope_tables(own_positions, HEAD_SIZE)
    scale_factor = 1.0 / math.sqrt(HEAD_SIZE)
    half_rows = half_devices * local_rows
    query_positions = lax.dynamic_slice_in_dim(all_positions, my_half * half_rows, half_rows)
    allowed = all_positions[None, :] <= query_positions[:, None]
    half_select = (jnp.arange(halves, dtype=jnp.int32) == my_half)[:, None, None, None]

    def to_heads(per_head):
        by_head = jnp.transpose(per_head, (1, 0, 2))
        return jnp.where(half_select, by_head[None], jnp.zeros_like(by_head)[None]).reshape(
            ctx_size, local_rows, per_head.shape[-1]
        )

    def gather_half(received):
        return lax.dynamic_slice_in_dim(received, my_half * half_devices, half_devices, 0).reshape(
            half_rows, received.shape[-1]
        )

    def from_heads(per_head):
        blocks = per_head.reshape(half_devices, local_rows, per_head.shape[-1])
        return jnp.where(half_select, blocks[None], jnp.zeros_like(blocks)[None]).reshape(
            ctx_size, local_rows, per_head.shape[-1]
        )

    def own_heads(received):
        mine = lax.dynamic_slice_in_dim(received, my_half * half_devices, half_devices, 0)
        return jnp.transpose(mine, (1, 0, 2))

    def exchange(values):
        return lax.all_to_all(values, CTX, split_axis=0, concat_axis=0, tiled=True)

    full_query, full_key, full_value, full_output, full_gate, full_up, full_down = (
        gather_fsdp(query_weight),
        gather_fsdp(key_projection),
        gather_fsdp(value_projection),
        gather_fsdp(output_weight),
        gather_fsdp(gate_weight),
        gather_fsdp(up_weight),
        gather_fsdp(down_weight),
    )
    input_f32 = layer_input[0].astype(jnp.float32)
    gained, first_normed, first_scale = rms_apply(input_f32, first_gain)
    attention_input = gained.astype(jnp.bfloat16)
    query_pre = jnp.dot(attention_input, full_query, preferred_element_type=jnp.float32).reshape(
        local_rows, HQ, HEAD_SIZE
    )
    query_gained, query_normed, query_scale = rms_apply(query_pre, query_gain)
    query_rotated = rotary_apply(query_gained, cosine_table, sine_values_table).astype(jnp.bfloat16)
    key_before_norm = jnp.dot(
        attention_input, full_key, preferred_element_type=jnp.float32
    ).reshape(local_rows, KEY_VALUE_HEADS, HEAD_SIZE)
    key_after_gain, key_after_norm, key_norm_scale = rms_apply(key_before_norm, key_norm_gain)
    own_keys = rotary_apply(key_after_gain, cosine_table, sine_values_table).astype(jnp.bfloat16)
    own_values = (
        jnp.dot(attention_input, full_value, preferred_element_type=jnp.float32)
        .astype(jnp.bfloat16)
        .reshape(local_rows, KEY_VALUE_HEADS, HEAD_SIZE)
    )
    group = HQ // KEY_VALUE_HEADS
    key_value = jnp.repeat(jnp.concatenate([own_keys, own_values], axis=-1), group, axis=1)
    sent = jnp.concatenate(
        [to_heads(query_rotated), jnp.tile(jnp.transpose(key_value, (1, 0, 2)), (halves, 1, 1))],
        axis=-1,
    )
    received = exchange(sent)
    head_query = gather_half(received[..., :HEAD_SIZE])
    head_key = received[..., HEAD_SIZE : 2 * HEAD_SIZE].reshape(-1, HEAD_SIZE)
    head_value = received[..., 2 * HEAD_SIZE :].reshape(-1, HEAD_SIZE)

    def head_scores():
        raw_scores = (
            jnp.einsum("qd,kd->qk", head_query, head_key, preferred_element_type=jnp.float32)
            * scale_factor
        )
        return jnp.where(allowed, raw_scores, MASKED)

    raw_scores = head_scores()
    row_max = jnp.max(raw_scores, axis=-1, keepdims=True)
    log_total = row_max + jnp.log(jnp.sum(jnp.exp(raw_scores - row_max), axis=-1, keepdims=True))
    weights_b = jnp.exp(raw_scores - log_total).astype(jnp.bfloat16)
    head_mixed = jnp.dot(weights_b, head_value, preferred_element_type=jnp.float32)
    mixed_b = own_heads(exchange(from_heads(head_mixed.astype(jnp.bfloat16)))).reshape(
        local_rows, HQ * HEAD_SIZE
    )
    residual_mid = input_f32 + jnp.dot(mixed_b, full_output, preferred_element_type=jnp.float32)
    gained_mid, second_normed, second_scale = rms_apply(residual_mid, second_gain)
    mlp_in = gained_mid.astype(jnp.bfloat16)
    gate_pre = jnp.dot(mlp_in, full_gate, preferred_element_type=jnp.float32)
    up_pre = jnp.dot(mlp_in, full_up, preferred_element_type=jnp.float32)
    sigmoid_gate = jax.nn.sigmoid(gate_pre)
    silu_gate = gate_pre * sigmoid_gate
    hidden = (silu_gate * up_pre).astype(jnp.bfloat16)
    layer_output = (
        residual_mid + jnp.dot(hidden, full_down, preferred_element_type=jnp.float32)
    ).astype(jnp.bfloat16)
    own_cotangent = cotangent[0]
    hidden_grad = right_dot(own_cotangent, full_down)
    gate_grad = (
        hidden_grad * up_pre * sigmoid_gate * (1.0 + gate_pre * (1.0 - sigmoid_gate))
    ).astype(jnp.bfloat16)
    up_grad = (hidden_grad * silu_gate).astype(jnp.bfloat16)
    mlp_in_grad = right_dot(gate_grad, full_gate) + right_dot(up_grad, full_up)
    second_gain_grad = jnp.sum(mlp_in_grad * second_normed, axis=0)
    mid_grad = own_cotangent.astype(jnp.float32) + root_mean_square_backward(
        mlp_in_grad, second_normed, second_scale, second_gain
    )
    mid_grad_b = mid_grad.astype(jnp.bfloat16)
    mixed_gradient = right_dot(mid_grad_b, full_output).astype(jnp.bfloat16)
    head_out_grad = gather_half(
        exchange(to_heads(mixed_gradient.reshape(local_rows, HQ, HEAD_SIZE)))
    )
    out_grad_f = head_out_grad.astype(jnp.float32)
    delta = jnp.sum(out_grad_f * head_mixed, axis=-1, keepdims=True)
    probabilities = jnp.exp(head_scores() - log_total)
    value_part = left_dot(probabilities.astype(jnp.bfloat16), head_out_grad)
    prob_grad = right_dot(head_out_grad, head_value)
    score_grad = (probabilities * (prob_grad - delta)).astype(jnp.bfloat16)
    query_part = jnp.dot(score_grad, head_key, preferred_element_type=jnp.float32) * scale_factor
    key_part = left_dot(score_grad, head_query) * scale_factor
    returned = exchange(
        jnp.concatenate(
            [
                from_heads(query_part.astype(jnp.bfloat16)),
                jnp.concatenate([key_part, value_part], axis=-1)
                .astype(jnp.bfloat16)
                .reshape(ctx_size, local_rows, 2 * HEAD_SIZE),
            ],
            axis=-1,
        )
    )
    query_grad_rows = own_heads(returned[..., :HEAD_SIZE]).astype(jnp.float32)
    kv_parts = (
        returned[..., HEAD_SIZE:]
        .astype(jnp.float32)
        .reshape(halves, KEY_VALUE_HEADS, group, local_rows, 2 * HEAD_SIZE)
    )
    kv_grad = jnp.transpose(jnp.sum(kv_parts, axis=(0, 2)), (1, 0, 2))
    local_key_gradient = kv_grad[..., :HEAD_SIZE]
    own_value_grad = kv_grad[..., HEAD_SIZE:].reshape(local_rows, KEY_VALUE_HEADS * HEAD_SIZE)
    query_back = rotary_backward(query_grad_rows, cosine_table, sine_values_table)
    query_gain_grad = jnp.sum(query_back * query_normed, axis=(0, 1))
    query_pre_grad = (
        root_mean_square_backward(query_back, query_normed, query_scale, query_gain)
        .astype(jnp.bfloat16)
        .reshape(local_rows, HQ * HEAD_SIZE)
    )
    key_backward_pass = rotary_backward(local_key_gradient, cosine_table, sine_values_table)
    key_gain_grad = jnp.sum(key_backward_pass * key_after_norm, axis=(0, 1))
    key_before_norm_gradient = (
        root_mean_square_backward(key_backward_pass, key_after_norm, key_norm_scale, key_norm_gain)
        .astype(jnp.bfloat16)
        .reshape(local_rows, KEY_VALUE_HEADS * HEAD_SIZE)
    )
    value_gradient_second = own_value_grad.astype(jnp.bfloat16)
    attn_in_grad = (
        right_dot(query_pre_grad, full_query)
        + right_dot(key_before_norm_gradient, full_key)
        + right_dot(value_gradient_second, full_value)
    )
    first_gain_grad = jnp.sum(attn_in_grad * first_normed, axis=0)
    input_grad = mid_grad + root_mean_square_backward(
        attn_in_grad, first_normed, first_scale, first_gain
    )
    attn_cols, mixed_cols, mlp_cols, hidden_cols = (
        lax.all_to_all(attention_input, FSDP, split_axis=1, concat_axis=0, tiled=True),
        lax.all_to_all(mixed_b, FSDP, split_axis=1, concat_axis=0, tiled=True),
        lax.all_to_all(mlp_in, FSDP, split_axis=1, concat_axis=0, tiled=True),
        lax.all_to_all(hidden, FSDP, split_axis=1, concat_axis=0, tiled=True),
    )
    cot_rows, gate_rows, up_rows, mid_rows, query_rows, key_rows, value_row_block = (
        gather_fsdp(own_cotangent),
        gather_fsdp(gate_grad),
        gather_fsdp(up_grad),
        gather_fsdp(mid_grad_b),
        gather_fsdp(query_pre_grad),
        gather_fsdp(key_before_norm_gradient),
        gather_fsdp(value_gradient_second),
    )
    query_shard = left_dot(attn_cols, query_rows)
    key_shard = left_dot(attn_cols, key_rows)
    value_shard = left_dot(attn_cols, value_row_block)
    output_shard = left_dot(mixed_cols, mid_rows)
    gate_shard = left_dot(mlp_cols, gate_rows)
    up_shard = left_dot(mlp_cols, up_rows)
    down_shard = left_dot(hidden_cols, cot_rows)
    first_shard, second_shard, query_gain_shard, key_gain_shard = (
        lax.psum_scatter(first_gain_grad, FSDP, scatter_dimension=0, tiled=True),
        lax.psum_scatter(second_gain_grad, FSDP, scatter_dimension=0, tiled=True),
        lax.psum_scatter(query_gain_grad, FSDP, scatter_dimension=0, tiled=True),
        lax.psum_scatter(key_gain_grad, FSDP, scatter_dimension=0, tiled=True),
    )
    shards = (
        query_shard,
        key_shard,
        value_shard,
        output_shard,
        gate_shard,
        up_shard,
        down_shard,
        first_shard,
        second_shard,
        query_gain_shard,
        key_gain_shard,
    )
    totals = reduce_ctx(shards)
    (
        query_total,
        key_total,
        value_total,
        output_total,
        gate_total,
        up_total,
        down_total,
        first_total,
        second_total,
        query_gain_total,
        key_gain_total,
    ) = totals
    return (
        layer_output[None],
        input_grad[None],
        query_total,
        key_total,
        value_total,
        output_total,
        gate_total,
        up_total,
        down_total,
        first_total,
        second_total,
        query_gain_total,
        key_gain_total,
    )


def solution(mesh):
    in_specs = (
        P(FSDP, CTX, None),
        P(FSDP, CTX, None),
        P(FSDP, None),
        P(FSDP, None),
        P(FSDP, None),
        P(FSDP, None),
        P(FSDP, None),
        P(FSDP, None),
        P(FSDP, None),
        P(FSDP, None),
        P(),
        P(),
        P(),
        P(),
    )
    out_specs = (
        P(FSDP, CTX, None),
        P(FSDP, CTX, None),
        P(FSDP, None),
        P(FSDP, None),
        P(FSDP, None),
        P(FSDP, None),
        P(FSDP, None),
        P(FSDP, None),
        P(FSDP, None),
        P(FSDP),
        P(FSDP),
        P(FSDP),
        P(FSDP),
    )
    torus_mesh = jax.sharding.Mesh(mesh.devices.reshape(2, 4, 4, 2, 2), ("yh", "x", "z", "yl", "c"))
    return jax.shard_map(
        on_device, mesh=torus_mesh, in_specs=in_specs, out_specs=out_specs, check_vma=False
    )
```

profile of v0, /device:TPU:1, one launch (start us, length us, event | category | flops | bytes accessed | tf_op | source)
XLA Modules:
  0.0 1240.5 jit_solution(9010868726562113697)
XLA Ops:
  11.2 25.6 %all-gather.61.cloned.1.call-done = bf16[512,1024]{1,0:T(8,128)(2,1)} async-done(((bf16[256,1024]{1,0:T(8,128)(2,1)}), bf16[512,1024]{1,0:T(8,128)(2,1)}) %all-gather.61.cloned.1.call-update) | async-done | bytes 1048592 | tf_op jit(solution)/shard_map/all_gather | solution.py:76
  36.8 26.4 %all-gather.65.cloned.1.call-done = bf16[512,1024]{1,0:T(8,128)(2,1)} async-done(((bf16[256,1024]{1,0:T(8,128)(2,1)}), bf16[512,1024]{1,0:T(8,128)(2,1)}) %all-gather.65.cloned.1.call-update) | async-done | bytes 1048592 | tf_op jit(solution)/shard_map/all_gather | solution.py:76
  63.3 38.2 %all-gather.57.cloned.1.call-done = bf16[512,2048]{1,0:T(8,128)(2,1)} async-done(((bf16[256,2048]{1,0:T(8,128)(2,1)}), bf16[512,2048]{1,0:T(8,128)(2,1)}) %all-gather.57.cloned.1.call-update) | async-done | bytes 2097168 | tf_op jit(solution)/shard_map/all_gather | solution.py:76
  102.2 37.5 %all-gather.69.cloned.1.call-done = bf16[1024,1024]{1,0:T(8,128)(2,1)} async-done(((bf16[512,1024]{1,0:T(8,128)(2,1)}), bf16[1024,1024]{1,0:T(8,128)(2,1)}) %all-gather.69.cloned.1.call-update) | async-done | bytes 2097168 | tf_op jit(solution)/shard_map/all_gather | solution.py:76
  139.8 49.9 %all-gather.73.cloned.1.call-done = bf16[512,3072]{1,0:T(8,128)(2,1)} async-done(((bf16[256,3072]{1,0:T(8,128)(2,1)}), bf16[512,3072]{1,0:T(8,128)(2,1)}) %all-gather.73.cloned.1.call-update) | async-done | bytes 3145744 | tf_op jit(solution)/shard_map/all_gather | solution.py:76
  190.3 49.3 %all-gather.77.cloned.1.call-done = bf16[512,3072]{1,0:T(8,128)(2,1)} async-done(((bf16[256,3072]{1,0:T(8,128)(2,1)}), bf16[512,3072]{1,0:T(8,128)(2,1)}) %all-gather.77.cloned.1.call-update) | async-done | bytes 3145744 | tf_op jit(solution)/shard_map/all_gather | solution.py:76
  239.9 16.1 %all-gather.63.cloned.1.call-done = bf16[2,512,1024]{2,1,0:T(8,128)(2,1)} async-done(((bf16[2,256,1024]{2,1,0:T(8,128)(2,1)}), bf16[2,512,1024]{2,1,0:T(8,128)(2,1)}) %all-gather.63.cloned.1.call-update) | async-done | bytes 2097168 | tf_op jit(solution)/shard_map/all_gather | solution.py:77
  256.0 2.9 copy.80
  261.1 11.2 all-gather.67.cloned.1.call-done
  278.2 13.5 %all-gather.59.cloned.1.call-done = bf16[2,512,2048]{2,1,0:T(8,128)(2,1)} async-done(((bf16[2,256,2048]{2,1,0:T(8,128)(2,1)}), bf16[2,512,2048]{2,1,0:T(8,128)(2,1)}) %all-gather.59.cloned.1.call-update) | async-done | bytes 4194320 | tf_op jit(solution)/shard_map/all_gather | solution.py:77
  291.7 6.4 copy.79
  298.1 3.5 multiply_reduce_fusion.3
  305.8 3.5 pad_maximum_fusion
  309.3 9.6 all-to-all-start
  319.2 56.7 %all-gather.81.cloned.1.call-done = bf16[1536,1024]{1,0:T(8,128)(2,1)} async-done(((bf16[768,1024]{1,0:T(8,128)(2,1)}), bf16[1536,1024]{1,0:T(8,128)(2,1)}) %all-gather.81.cloned.1.call-update) | async-done | bytes 3145744 | tf_op jit(solution)/shard_map/all_gather | solution.py:76
  378.2 14.4 %fusion.49 = (f32[2048]{0:T(1024)S(1)}, f32[2048,4096]{1,0:T(8,128)}) fusion(s32[2048]{0:T(1024)S(1)} %dynamic_slice.18, s32[4096]{0:T(1024)S(1)} %add.146, bf16[2048,128]{1,0:T(8,128)(2,1)S(1)} %bitcast.313, bf16[4096,128]{1,0:T(8,128)(2,1)S(1)} %bitcast.307), kind=kOutput, calls=%fused_computation.148 | convolution fusion | flops 2181036032 | bytes 35160064 | tf_op jit(solution)/shard_map/qd,kd->qk/dot_general | solution.py:199
  392.6 16.1 %exponential_reduce_fusion = f32[2048]{0:T(1024)S(1)} fusion(f32[2048]{0:T(1024)S(1)} %get-tuple-element.56, f32[2048,4096]{1,0:T(8,128)} %get-tuple-element.57, s32[2048]{0:T(1024)S(1)} %dynamic_slice.18, s32[4096]{0:T(1024)S(1)} %add.146), kind=kLoop, calls=%fused_computation.6 | loop fusion | flops 41940992 | bytes 33595392 | tf_op jit(solution)/shard_map/reduce_sum | solution.py:206
  408.7 18.5 %fusion.51 = (bf16[2048,128]{1,0:T(8,128)(2,1)S(1)}, f32[2048,128]{1,0:T(8,128)}) fusion(bf16[4096,128]{1,0:T(8,128)(2,1)S(1)} %bitcast.309, f32[2048]{0:T(1024)S(1)} %log_add_fusion, f32[2048,4096]{1,0:T(8,128)} %get-tuple-element.57, s32[2048]{0:T(1024)S(1)} %dynamic_slice.18, s32[4096]{0:T(1024)S(1)} %add.146), kind=kOutput, calls=%fused_computation.150 | convolution fusion | flops 2189688832 | bytes 36208640 | tf_op jit(solution)/shard_map/dot_general | solution.py:208
  427.6 28.8 %all_to_all.93 = bf16[32,128,128]{1,2,0:T(8,128)(2,1)S(1)} all-to-all(bf16[32,128,128]{1,2,0:T(8,128)(2,1)S(1)} %bitcast_select_fusion.3), channel_id=1, replica_groups=mesh['yh'=2,'x'=4,'z'=4,'yl'=2,'c'=2] {'yh','x','z'}, dimensions={0} | all-to-all | bytes 2097152 | tf_op jit(solution)/shard_map/all_to_all | solution.py:157
  456.5 3.7 multiply_reduce_fusion.8
  460.4 6.0 fusion.52
  466.4 5.0 fusion.53
  471.3 7.5 multiply_convert_fusion.1
  478.9 6.1 fusion.54
  484.9 5.6 multiply_reduce_fusion.5
  497.6 5.5 all-to-all-start.2
  503.5 20.3 %fusion.2 = bf16[4096,2048]{0,1:T(8,128)(2,1)} fusion(f32[2048,4096]{1,0:T(8,128)} %get-tuple-element.57, f32[2048]{0:T(1024)S(1)} %log_add_fusion, s32[4096]{0:T(1024)S(1)} %add.146, s32[2048]{0:T(1024)S(1)} %dynamic_slice.18), kind=kLoop, calls=%fused_computation.3 | loop fusion | flops 41943040 | bytes 50364416 | tf_op jit(solution)/shard_map/convert_element_type | solution.py:207
  523.8 22.6 %copy.81 = bf16[4096,2048]{1,0:T(8,128)(2,1)} copy(bf16[4096,2048]{0,1:T(8,128)(2,1)} %fusion.2) | data formatting | bytes 33554432 | tf_op jit(solution)/shard_map/dot_general | solution.py:64
  551.3 20.5 %multiply_convert_fusion = bf16[2048,4096]{1,0:T(8,128)(2,1)} fusion(f32[2048]{0:T(1024)S(1)} %multiply_reduce_fusion.2, f32[2048]{0:T(1024)S(1)} %log_add_fusion, bf16[2048,128]{1,0:T(8,128)(2,1)S(1)} %bitcast.265, bf16[4096,128]{1,0:T(8,128)(2,1)} %bitcast.310, f32[2048,4096]{1,0:T(8,128)} %get-tuple-element.57, s32[2048]{0:T(1024)S(1)} %dynamic_slice.18, ...), kind=kOutput, calls=%fused_computation.4 | convolution fusion | flops 2206203904 | bytes 51945472 | tf_op jit(solution)/shard_map/dot_general | solution.py:70
  571.7 9.3 fusion.8
  582.7 5.8 fusion.7
  595.0 10.3 convolution_convert_fusion.6
  605.3 3.2 pad_maximum_fusion.1
  608.4 9.3 all-to-all-start.3
  618.4 44.4 %all_gather.212 = bf16[2,128,1024]{2,1,0:T(8,128)(2,1)} all-gather(bf16[1,128,1024]{2,1,0:T(8,128)(2,1)S(1)} %copy-done.15), channel_id=1, replica_groups=mesh['yh'=2,'x'=4,'z'=4,'yl'=2,'c'=2] {'yl'}, dimensions={0}, use_global_device_ids=true | all-gather | bytes 786432 | tf_op jit(solution)/shard_map/all_gather | solution.py:76
  668.0 10.4 all-gather.17
  683.1 6.5 all_gather.194
  691.7 9.3 all-to-all-start.7
  702.2 22.3 %all_gather.197 = bf16[2,128,1024]{2,1,0:T(8,128)(2,1)} all-gather(bf16[1,128,1024]{2,1,0:T(8,128)(2,1)S(1)} %copy.74), channel_id=1, replica_groups=mesh['yh'=2,'x'=4,'z'=4,'yl'=2,'c'=2] {'yl'}, dimensions={0}, use_global_device_ids=true | all-gather | bytes 786432 | tf_op jit(solution)/shard_map/all_gather | solution.py:76
  725.8 6.1 all-to-all-start.5
  735.4 2.5 fusion.12
  740.0 4.2 all-to-all-start.6
  744.2 2.8 all-gather.91.cloned.1.call-done
  754.7 9.4 all-reduce.5
  764.4 5.7 all-to-all-start.4
  770.1 2.9 fusion.10
  774.4 8.2 all-gather.99.cloned.1.call-done
  782.7 2.9 fusion.11
  787.1 10.4 all-gather.87.cloned.1.call-done
  800.0 12.2 all-gather.89.cloned.1.call-done
  815.0 13.3 %all-gather.85.cloned.1.call-done = bf16[2,256,2048]{2,1,0:T(8,128)(2,1)} async-done(((bf16[2,128,2048]{2,1,0:T(8,128)(2,1)}), bf16[2,256,2048]{2,1,0:T(8,128)(2,1)}) %all-gather.85.cloned.1.call-update) | async-done | bytes 2097168 | tf_op jit(solution)/shard_map/all_gather | solution.py:77
  832.0 103.5 %concatenate.38 = bf16[3932736]{0:T(1024)(128)(2,1)} concatenate(bf16[524288]{0:T(1024)(128)(2,1)} %bitcast.272, bf16[262144]{0:T(1024)(128)(2,1)} %bitcast.291, bf16[262144]{0:T(1024)(128)(2,1)} %bitcast.292, bf16[524288]{0:T(1024)(128)(2,1)S(1)} %bitcast.271, bf16[786432]{0:T(1024)(128)(2,1)} %bitcast.261, bf16[786432]{0:T(1024)(128)(2,1)} %bitcast.262, ...), dimensions={0} | concatenate | bytes 15730944 | tf_op jit(solution)/shard_map/concatenate | solution.py:82
  935.5 8.3 pad_bitcast_fusion
  943.9 78.1 %reduce-scatter.3.cloned.1.call-done = bf16[7744,128]{1,0:T(8,128)(2,1)} async-done(((bf16[30976,128]{1,0:T(8,128)(2,1)}), bf16[7744,128]{1,0:T(8,128)(2,1)}) %reduce-scatter.3.cloned.1.call-update) | async-done | bytes 1982480 | tf_op jit(solution)/shard_map/reduce_scatter | solution.py:87
  1022.0 30.6 %reduce-scatter.5.cloned.1.call-done = bf16[1936,128]{1,0:T(8,128)(2,1)} async-done(((bf16[7744,128]{1,0:T(8,128)(2,1)}), bf16[1936,128]{1,0:T(8,128)(2,1)}) %reduce-scatter.5.cloned.1.call-update) | async-done | bytes 495632 | tf_op jit(solution)/shard_map/reduce_scatter | solution.py:88
  1052.7 37.9 %all-reduce.8.cloned.1.call-done = bf16[1936,128]{1,0:T(8,128)(2,1)} async-done(((bf16[1936,128]{1,0:T(8,128)(2,1)}), bf16[1936,128]{1,0:T(8,128)(2,1)}) %all-reduce.8.cloned.1.call-update) | async-done | bytes 495632 | tf_op jit(solution)/shard_map/psum | solution.py:89
  1091.0 31.0 %all-gather.53.cloned.1.call-done = bf16[7744,128]{1,0:T(8,128)(2,1)} async-done(((bf16[1936,128]{1,0:T(8,128)(2,1)}), bf16[7744,128]{1,0:T(8,128)(2,1)}) %all-gather.53.cloned.1.call-update) | async-done | bytes 1982480 | tf_op jit(solution)/shard_map/all_gather | solution.py:90
  1122.0 4.6 fusion.21
  1127.7 75.5 %all-gather.55.cloned.1.call-done = bf16[30976,128]{1,0:T(8,128)(2,1)} async-done(((bf16[7744,128]{1,0:T(8,128)(2,1)}), bf16[30976,128]{1,0:T(8,128)(2,1)}) %all-gather.55.cloned.1.call-update) | async-done | bytes 7929872 | tf_op jit(solution)/shard_map/all_gather | solution.py:91
  1203.3 5.7 slice_convert_fusion
  1208.9 4.5 reshape.471
  1213.4 4.5 reshape.472
  1220.2 3.1 slice_convert_fusion.3
  1223.3 2.7 reshape.467
  (255 shorter events, 91.7 us)
Async XLA Ops:
  7.2 29.6 %all-gather.61.cloned.1.call-start = ((), (), s32[]{:S(2)}) async-start(), calls=%async_computation.18 | async-start | bytes 1572864 | tf_op jit(solution)/shard_map/all_gather | solution.py:76
  7.9 55.3 %all-gather.65.cloned.1.call-start = ((), (), s32[]{:S(2)}) async-start(), calls=%async_computation.20 | async-start | bytes 1572864 | tf_op jit(solution)/shard_map/all_gather | solution.py:76
  8.7 92.9 %all-gather.57.cloned.1.call-start = ((), (), s32[]{:S(2)}) async-start(), calls=%async_computation.16 | async-start | bytes 3145728 | tf_op jit(solution)/shard_map/all_gather | solution.py:76
  9.4 130.3 %all-gather.69.cloned.1.call-start = ((), (), s32[]{:S(2)}) async-start(), calls=%async_computation.22 | async-start | bytes 3145728 | tf_op jit(solution)/shard_map/all_gather | solution.py:76
  10.0 179.7 %all-gather.73.cloned.1.call-start = ((), (), s32[]{:S(2)}) async-start(), calls=%async_computation.24 | async-start | bytes 4718592 | tf_op jit(solution)/shard_map/all_gather | solution.py:76
  10.6 229.1 %all-gather.77.cloned.1.call-start = ((), (), s32[]{:S(2)}) async-start(), calls=%async_computation.26 | async-start | bytes 4718592 | tf_op jit(solution)/shard_map/all_gather | solution.py:76
  11.1 244.9 %all-gather.63.cloned.1.call-start = ((), (), s32[]{:S(2)}) async-start(), calls=%async_computation.19 | async-start | bytes 3145728 | tf_op jit(solution)/shard_map/all_gather | solution.py:77
  36.8 235.6 %all-gather.67.cloned.1.call-start = ((), (), s32[]{:S(2)}) async-start(), calls=%async_computation.21 | async-start | bytes 3145728 | tf_op jit(solution)/shard_map/all_gather | solution.py:77
  63.3 228.5 %all-gather.59.cloned.1.call-start = ((), (), s32[]{:S(2)}) async-start(), calls=%async_computation.17 | async-start | bytes 6291456 | tf_op jit(solution)/shard_map/all_gather | solution.py:77
  101.5 88.4 %copy-start.37 = (s32[1,64]{1,0:T(1,128)S(1)}, s32[1,64]{1,0:T(1,128)}, u32[]{:S(2)}) copy-start(s32[1,64]{1,0:T(1,128)} %param.16) | copy-start | bytes 772
  101.5 88.7 %copy-start = (bf16[1,128,1024]{2,1,0:T(8,128)(2,1)S(1)}, bf16[1,128,1024]{2,1,0:T(8,128)(2,1)}, u32[]{:S(2)}) copy-start(bf16[1,128,1024]{2,1,0:T(8,128)(2,1)} %param.14) | copy-start | bytes 786436
  101.6 274.4 %all-gather.81.cloned.1.call-start = ((), (), s32[]{:S(2)}) async-start(), calls=%async_computation.28 | async-start | bytes 4718592 | tf_op jit(solution)/shard_map/all_gather | solution.py:76
  102.2 354.4 %all-gather.71.cloned.1.call-start = ((), (), s32[]{:S(2)}) async-start(), calls=%async_computation.23 | async-start | bytes 6291456 | tf_op jit(solution)/shard_map/all_gather | solution.py:77
  139.7 320.7 %all-gather.75.cloned.1.call-start = ((), (), s32[]{:S(2)}) async-start(), calls=%async_computation.25 | async-start | bytes 9437184 | tf_op jit(solution)/shard_map/all_gather | solution.py:77
  189.7 69.2 %copy-start.27 = (f32[1024]{0:T(1024)S(1)}, f32[1024]{0:T(1024)}, u32[]{:S(2)}) copy-start(f32[1024]{0:T(1024)} %param.24) | copy-start | bytes 12292
  189.7 276.7 %all-gather.79.cloned.1.call-start = ((), (), s32[]{:S(2)}) async-start(), calls=%async_computation.27 | async-start | bytes 9437184 | tf_op jit(solution)/shard_map/all_gather | solution.py:77
  239.7 20.8 %copy-start.34 = (f32[128]{0:T(128)S(1)}, f32[128]{0:T(128)}, u32[]{:S(2)}) copy-start(f32[128]{0:T(128)} %param.27) | copy-start | bytes 1540
  239.7 58.4 %copy-start.32 = (f32[128]{0:T(128)}, f32[128]{0:T(128)S(1)}, u32[]{:S(2)}) copy-start(f32[128]{0:T(128)S(1)} %add_rsqrt_fusion.3) | copy-start | bytes 1540
  259.7 15.7 %copy-start.30 = (f32[128,8]{0,1:T(8,128)}, f32[128,8]{0,1:T(8,128)S(1)}, u32[]{:S(2)}) copy-start(f32[128,8]{0,1:T(8,128)S(1)} %add_rsqrt_fusion.1) | copy-start | bytes 12292
  309.3 66.7 %all-to-all-start = ((bf16[32,128,384]{2,1,0:T(8,128)(2,1)}), bf16[32,128,384]{2,1,0:T(8,128)(2,1)}, u32[]{:S(2)}, u32[]{:S(2)}) async-start(bf16[32,128,384]{2,1,0:T(8,128)(2,1)} %pad_maximum_fusion), calls=%async_computation | async-start | bytes 6291456 | tf_op jit(solution)/shard_map/all_to_all | solution.py:157
  318.9 152.4 %all-gather.83.cloned.1.call-start = ((), (), s32[]{:S(2)}) async-start(), calls=%async_computation.29 | async-start | bytes 9437184 | tf_op jit(solution)/shard_map/all_gather | solution.py:77
  378.1 14.5 %copy-start.22 = (bf16[32,128,128]{2,1,0:T(8,128)(2,1)}, bf16[32,128,128]{2,1,0:T(8,128)(2,1)S(1)}, u32[]{:S(2)}) copy-start(bf16[32,128,128]{2,1,0:T(8,128)(2,1)S(1)} %get-tuple-element.39) | copy-start | bytes 3145732
  378.1 30.6 %copy-start.24 = (bf16[32,128,128]{2,1,0:T(8,128)(2,1)}, bf16[32,128,128]{2,1,0:T(8,128)(2,1)S(1)}, u32[]{:S(2)}) copy-start(bf16[32,128,128]{2,1,0:T(8,128)(2,1)S(1)} %get-tuple-element.40) | copy-start | bytes 3145732
  378.2 14.4 %copy-start.25 = (bf16[16,128,128]{2,1,0:T(8,128)(2,1)}, bf16[16,128,128]{2,1,0:T(8,128)(2,1)S(1)}, u32[]{:S(2)}) copy-start(bf16[16,128,128]{2,1,0:T(8,128)(2,1)S(1)} %constant_dynamic-slice_fusion.2) | copy-start | bytes 1572868
  427.6 32.6 %copy-start.29 = (f32[1024]{0:T(1024)S(1)}, f32[1024]{0:T(1024)}, u32[]{:S(2)}) copy-start(f32[1024]{0:T(1024)} %param.25) | copy-start | bytes 12292
  466.4 5.0 copy-start.15
  484.9 5.8 copy-start.2
  490.5 4.9 copy-start.9
  497.6 48.9 %all-to-all-start.2 = ((bf16[32,128,128]{1,2,0:T(8,128)(2,1)}), bf16[32,128,128]{1,2,0:T(8,128)(2,1)}, u32[]{:S(2)}, u32[]{:S(2)}) async-start(bf16[32,128,128]{1,2,0:T(8,128)(2,1)} %bitcast_select_fusion.2), calls=%async_computation.2 | async-start | bytes 2097152 | tf_op jit(solution)/shard_map/all_to_all | solution.py:157
  503.1 175.5 %all-gather.93.cloned.1.call-start = ((), (), s32[]{:S(2)}) async-start(), calls=%async_computation.34 | async-start | bytes 2359296 | tf_op jit(solution)/shard_map/all_gather | solution.py:76
  551.3 20.5 %copy-start.23 = (bf16[32,128,128]{2,1,0:T(8,128)(2,1)S(1)}, bf16[32,128,128]{2,1,0:T(8,128)(2,1)}, u32[]{:S(2)}) copy-start(bf16[32,128,128]{2,1,0:T(8,128)(2,1)} %copy-done.22) | copy-start | bytes 3145732
  571.7 9.3 copy-start.26
  571.7 10.9 copy-start.39
  608.4 54.4 %all-to-all-start.3 = ((bf16[32,128,384]{1,2,0:T(8,128)(2,1)}), bf16[32,128,384]{1,2,0:T(8,128)(2,1)}, u32[]{:S(2)}, u32[]{:S(2)}) async-start(bf16[32,128,384]{1,2,0:T(8,128)(2,1)} %pad_maximum_fusion.1), calls=%async_computation.3 | async-start | bytes 6291456 | tf_op jit(solution)/shard_map/all_to_all | solution.py:157
  617.7 61.4 %all-gather.97.cloned.1.call-start = ((), (), s32[]{:S(2)}) async-start(), calls=%async_computation.36 | async-start | bytes 2359296 | tf_op jit(solution)/shard_map/all_gather | solution.py:76
  618.3 117.1 %all-gather.101.cloned.1.call-start = ((), (), s32[]{:S(2)}) async-start(), calls=%async_computation.38 | async-start | bytes 1572864 | tf_op jit(solution)/shard_map/all_gather | solution.py:77
  662.8 76.7 %all-gather.51.cloned.1.call-start = ((), (), s32[]{:S(2)}) async-start(), calls=%async_computation.10 | async-start | bytes 1572864 | tf_op jit(solution)/shard_map/all_gather | solution.py:76
  668.0 79.1 %all-gather.91.cloned.1.call-start = ((), (), s32[]{:S(2)}) async-start(), calls=%async_computation.33 | async-start | bytes 1572864 | tf_op jit(solution)/shard_map/all_gather | solution.py:77
  678.5 91.6 %all-gather.95.cloned.1.call-start = ((), (), s32[]{:S(2)}) async-start(), calls=%async_computation.35 | async-start | bytes 4718592 | tf_op jit(solution)/shard_map/all_gather | solution.py:77
  679.1 103.6 %all-gather.99.cloned.1.call-start = ((), (), s32[]{:S(2)}) async-start(), calls=%async_computation.37 | async-start | bytes 4718592 | tf_op jit(solution)/shard_map/all_gather | solution.py:77
  679.8 117.6 %all-gather.87.cloned.1.call-start = ((), (), s32[]{:S(2)}) async-start(), calls=%async_computation.31 | async-start | bytes 1572864 | tf_op jit(solution)/shard_map/all_gather | solution.py:77
  683.0 41.8 %copy-start.28 = (f32[1024]{0:T(1024)S(1)}, f32[1024]{0:T(1024)}, u32[]{:S(2)}) copy-start(f32[1024]{0:T(1024)} %param.24) | copy-start | bytes 12292
  689.6 42.3 %copy-start.33 = (f32[128]{0:T(128)S(1)}, f32[128]{0:T(128)}, u32[]{:S(2)}) copy-start(f32[128]{0:T(128)} %copy-done.32) | copy-start | bytes 1540
  691.7 41.1 %copy-start.38 = (u32[128]{0:T(128)S(1)}, u32[128]{0:T(128)}, u32[]{:S(2)}) copy-start(u32[128]{0:T(128)} %constant.90) | copy-start | bytes 1540
  691.7 34.1 %all-to-all-start.7 = ((bf16[128,4,768]{2,0,1:T(8,128)(2,1)}), bf16[128,4,768]{2,0,1:T(8,128)(2,1)}, u32[]{:S(2)}, u32[]{:S(2)}) async-start(bf16[128,4,768]{2,0,1:T(8,128)(2,1)} %bitcast.239), calls=%async_computation.7 | async-start | bytes 1572864 | tf_op jit(solution)/shard_map/all_to_all | solution.py:295
  701.0 111.2 %all-gather.89.cloned.1.call-start = ((), (), s32[]{:S(2)}) async-start(), calls=%async_computation.32 | async-start | bytes 1572864 | tf_op jit(solution)/shard_map/all_gather | solution.py:77
  702.1 33.4 %copy-start.19 = (bf16[128,8,128]{0,2,1:T(8,128)(2,1)}, bf16[128,8,128]{0,2,1:T(8,128)(2,1)S(1)}, u32[]{:S(2)}) copy-start(bf16[128,8,128]{0,2,1:T(8,128)(2,1)S(1)} %slice.169) | copy-start | bytes 786436
  725.8 14.2 %all-to-all-start.5 = ((bf16[128,4,512]{2,0,1:T(8,128)(2,1)}), bf16[128,4,512]{2,0,1:T(8,128)(2,1)}, u32[]{:S(2)}, u32[]{:S(2)}) async-start(bf16[128,4,512]{2,0,1:T(8,128)(2,1)} %copy.75), calls=%async_computation.5 | async-start | bytes 1048576 | tf_op jit(solution)/shard_map/all_to_all | solution.py:293
  731.9 96.5 %all-gather.85.cloned.1.call-start = ((), (), s32[]{:S(2)}) async-start(), calls=%async_computation.30 | async-start | bytes 3145728 | tf_op jit(solution)/shard_map/all_gather | solution.py:77
  737.9 12.7 %copy-start.5 = (bf16[2,512,1024]{2,1,0:T(8,128)(2,1)S(1)}, bf16[2,512,1024]{2,1,0:T(8,128)(2,1)}, u32[]{:S(2)}) copy-start(bf16[2,512,1024]{2,1,0:T(8,128)(2,1)} %all-gather.63.cloned.1.call-done) | copy-start | bytes 6291460
  740.0 24.4 %all-to-all-start.6 = ((bf16[128,4,256]{2,0,1:T(8,128)(2,1)}), bf16[128,4,256]{2,0,1:T(8,128)(2,1)S(1)}, u32[]{:S(2)}, u32[]{:S(2)}) async-start(bf16[128,4,256]{2,0,1:T(8,128)(2,1)} %bitcast.306), calls=%async_computation.6 | async-start | bytes 524288 | tf_op jit(solution)/shard_map/all_to_all | solution.py:294
  764.4 22.6 %all-to-all-start.4 = ((bf16[128,4,256]{2,0,1:T(8,128)(2,1)}), bf16[128,4,256]{2,0,1:T(8,128)(2,1)S(1)}, u32[]{:S(2)}, u32[]{:S(2)}) async-start(bf16[128,4,256]{2,0,1:T(8,128)(2,1)} %fusion.24), calls=%async_computation.4 | async-start | bytes 524288 | tf_op jit(solution)/shard_map/all_to_all | solution.py:292
  770.1 251.9 %reduce-scatter.3.cloned.1.call-start = ((), (), s32[]{:S(2)}) async-start(), calls=%async_computation.11 | async-start | bytes 9912320 | tf_op jit(solution)/shard_map/reduce_scatter | solution.py:87
  787.1 25.2 %copy-start.12 = (bf16[128,4,256]{2,0,1:T(8,128)(2,1)}, bf16[128,4,256]{2,0,1:T(8,128)(2,1)S(1)}, u32[]{:S(2)}) copy-start(bf16[128,4,256]{2,0,1:T(8,128)(2,1)S(1)} %all-to-all-done.4) | copy-start | bytes 786436
  812.2 19.8 %copy-start.7 = (bf16[96,8,8,128]{3,1,2,0:T(8,128)(2,1)S(1)}, bf16[96,8,8,128]{3,1,2,0:T(8,128)(2,1)}, u32[]{:S(2)}) copy-start(bf16[96,8,8,128]{3,1,2,0:T(8,128)(2,1)} %copy.93) | copy-start | bytes 4718596
  812.2 19.8 %copy-start.11 = (bf16[64,8,8,128]{3,1,2,0:T(8,128)(2,1)S(1)}, bf16[64,8,8,128]{3,1,2,0:T(8,128)(2,1)}, u32[]{:S(2)}) copy-start(bf16[64,8,8,128]{3,1,2,0:T(8,128)(2,1)} %copy.90) | copy-start | bytes 3145732
  943.8 178.1 %copy-start.14 = (bf16[128,3072]{1,0:T(8,128)(2,1)S(1)}, bf16[128,3072]{1,0:T(8,128)(2,1)}, u32[]{:S(2)}) copy-start(bf16[128,3072]{1,0:T(8,128)(2,1)} %get-tuple-element.38) | copy-start | bytes 2359300
  943.8 108.8 %reduce-scatter.5.cloned.1.call-start = ((), (), s32[]{:S(2)}) async-start(), calls=%async_computation.12 | async-start | bytes 2478080 | tf_op jit(solution)/shard_map/reduce_scatter | solution.py:88
  1022.0 68.6 %all-reduce.8.cloned.1.call-start = ((), (), s32[]{:S(2)}) async-start(), calls=%async_computation.13 | async-start | bytes 991232 | tf_op jit(solution)/shard_map/psum | solution.py:89
  1052.7 69.3 %all-gather.53.cloned.1.call-start = ((), (), s32[]{:S(2)}) async-start(), calls=%async_computation.14 | async-start | bytes 2478080 | tf_op jit(solution)/shard_map/all_gather | solution.py:90
  1090.7 112.6 %all-gather.55.cloned.1.call-start = ((), (), s32[]{:S(2)}) async-start(), calls=%async_computation.15 | async-start | bytes 9912320 | tf_op jit(solution)/shard_map/all_gather | solution.py:91
  1122.0 4.6 copy-start.10
  1122.0 4.6 copy-start.16
  1122.0 4.6 copy-start.21
  (12 other events, 32.1 us)
Sparse Core Ops, SparseCore 0:
  9.7 27.0 all-gather.60
  38.4 24.7 all-gather.64
  64.9 36.6 all-gather.56
  103.0 36.6 all-gather.68
  141.2 48.4 all-gather.72
  191.2 48.4 all-gather.76
  241.3 14.6 all-gather.62
  257.7 14.6 all-gather.66
  274.0 17.6 all-gather.58
  293.2 82.6 all-gather.80
  377.6 21.7 all-gather.70
  400.9 20.8 all-gather.74
  423.4 20.7 all-gather.78
  445.7 20.7 all-gather.82
  546.6 31.9 all-gather.92
  620.5 57.1 all-gather.96
  679.2 15.1 all-gather.100
  696.5 32.6 all-gather.50
  730.9 16.0 all-gather.90
  748.5 16.2 all-gather.94
  766.5 16.1 all-gather.98
  784.3 13.0 all-gather.86
  799.1 13.0 all-gather.88
  813.7 14.6 all-gather.84
  944.0 77.9 reduce-scatter.2
  1024.2 28.3 reduce-scatter.4
  1055.1 35.4 all-reduce.7
  1092.4 29.5 all-gather.52
  1123.7 79.5 all-gather.54
where the time goes:
time: 1260 us; the launch traced here: 1240 us
  waiting for transfers between devices  631 us (50%)
  local copies, waits for them, and re-layouts  204 us (16%)
  matrix products  146 us (12%)
  blocking collectives  122 us (10%)
  other arithmetic  69.1 us (5%)
  starting transfers between devices  51.6 us (4%)
  between operations  16.7 us (1%)
    all_gather x10, waiting for transfers between devices, gather_fsdp(): across = lax.all_gather(values, 'yl', axis=0, tiled=False)  284 us
    concatenate x1, local copies, waits for them, and re-layouts, reduce_ctx(): flat = jnp.concatenate([s.astype(jnp.bfloat16).reshape(-1) for s in shards])  104 us
    all_gather x14, waiting for transfers between devices, gather_fsdp(): both = lax.all_gather(across, 'c', axis=1, tiled=False)  87.8 us
    all_gather x4, blocking collectives, gather_fsdp(): across = lax.all_gather(values, 'yl', axis=0, tiled=False)  83.6 us
    reduce_scatter x1, waiting for transfers between devices, reduce_ctx(): part = lax.psum_scatter(flat, 'z', scatter_dimension=0, tiled=True)  78.1 us
    all_gather x1, waiting for transfers between devices, reduce_ctx(): full = lax.all_gather(part, 'z', axis=0, tiled=True).reshape(-1)  75.5 us
    dot_general x8, matrix products, right_dot(): lax.dot_general(left_side, right_side, (((1,), (1,)), ((), ())), preferre...  45.2 us
    psum x1, waiting for transfers between devices, reduce_ctx(): part = lax.psum(part, 'yh')  37.9 us
  transfers between devices with their start and end apart: 36, of which 21 were waited for; matrix products, arithmetic and copies ran while one was open for 20% of the time, Pallas kernels for 0%

commit v1 on v0

--- a/solution.py
+++ b/solution.py
@@ -86,7 +86,8 @@
     flat = jnp.pad(flat, (0, padded - flat.shape[0])).reshape(padded // lanes, lanes)
     part = lax.psum_scatter(flat, "z", scatter_dimension=0, tiled=True)
     part = lax.psum_scatter(part, "x", scatter_dimension=0, tiled=True)
-    part = lax.psum(part, "yh")
+    parts = lax.all_gather(part, "yh", axis=0, tiled=False)
+    part = parts.sum(axis=0)
     part = lax.all_gather(part, "x", axis=0, tiled=True)
     full = lax.all_gather(part, "z", axis=0, tiled=True).reshape(-1)
     out = []

time: 1260 us -> 1240 us (0.984)
  waiting for transfers between devices: 631 us -> 592 us
  blocking collectives: 122 us -> 137 us
    psum x1 -> x0, waiting for transfers between devices: 37.9 us -> none  [reduce_ctx(): part = lax.psum(part, 'yh')]
    all_gather x0 -> x1, blocking collectives: none -> 14.6 us  [reduce_ctx(): parts = lax.all_gather(part, 'yh', axis=0, tiled=False)]
  transfers between devices with their start and end apart: 36 -> 35, of which waited for: 21 -> 20; matrix products, arithmetic and copies ran while one was open for 20% -> 20% of each run, Pallas kernels for 0% -> 0%
where the time goes in v1:
time: 1240 us; the launch traced here: 1220 us
  waiting for transfers between devices  592 us (48%)
  local copies, waits for them, and re-layouts  205 us (17%)
  matrix products  146 us (12%)
  blocking collectives  137 us (11%)
  other arithmetic  70.1 us (6%)
  starting transfers between devices  51.4 us (4%)
  between operations  17 us (1%)
    all_gather x10, waiting for transfers between devices, gather_fsdp(): across = lax.all_gather(values, 'yl', axis=0, tiled=False)  284 us
    concatenate x1, local copies, waits for them, and re-layouts, reduce_ctx(): flat = jnp.concatenate([s.astype(jnp.bfloat16).reshape(-1) for s in shards])  104 us
    all_gather x14, waiting for transfers between devices, gather_fsdp(): both = lax.all_gather(across, 'c', axis=1, tiled=False)  87.8 us
    all_gather x4, blocking collectives, gather_fsdp(): across = lax.all_gather(values, 'yl', axis=0, tiled=False)  83.7 us
    reduce_scatter x1, waiting for transfers between devices, reduce_ctx(): part = lax.psum_scatter(flat, 'z', scatter_dimension=0, tiled=True)  78.1 us
    all_gather x1, waiting for transfers between devices, reduce_ctx(): full = lax.all_gather(part, 'z', axis=0, tiled=True).reshape(-1)  75.5 us
    dot_general x8, matrix products, right_dot(): lax.dot_general(left_side, right_side, (((1,), (1,)), ((), ())), preferre...  45.2 us
    dot_general x9, matrix products, left_dot(): lax.dot_general(left_side, right_side, (((0,), (0,)), ((), ())), preferre...  32.7 us
  transfers between devices with their start and end apart: 35, of which 20 were waited for; matrix products, arithmetic and copies ran while one was open for 20% of the time, Pallas kernels for 0%

profile of v1, /device:TPU:1, one launch (start us, length us, event | category | flops | bytes accessed | tf_op | source)
XLA Modules:
  0.0 1218.6 jit_solution(5021884124889565979)
XLA Ops:
  11.2 25.6 %all-gather.62.cloned.1.call-done = bf16[512,1024]{1,0:T(8,128)(2,1)} async-done(((bf16[256,1024]{1,0:T(8,128)(2,1)}), bf16[512,1024]{1,0:T(8,128)(2,1)}) %all-gather.62.cloned.1.call-update) | async-done | bytes 1048592 | tf_op jit(solution)/shard_map/all_gather | solution.py:76
  36.8 26.4 %all-gather.66.cloned.1.call-done = bf16[512,1024]{1,0:T(8,128)(2,1)} async-done(((bf16[256,1024]{1,0:T(8,128)(2,1)}), bf16[512,1024]{1,0:T(8,128)(2,1)}) %all-gather.66.cloned.1.call-update) | async-done | bytes 1048592 | tf_op jit(solution)/shard_map/all_gather | solution.py:76
  63.3 38.2 %all-gather.58.cloned.1.call-done = bf16[512,2048]{1,0:T(8,128)(2,1)} async-done(((bf16[256,2048]{1,0:T(8,128)(2,1)}), bf16[512,2048]{1,0:T(8,128)(2,1)}) %all-gather.58.cloned.1.call-update) | async-done | bytes 2097168 | tf_op jit(solution)/shard_map/all_gather | solution.py:76
  102.2 37.5 %all-gather.70.cloned.1.call-done = bf16[1024,1024]{1,0:T(8,128)(2,1)} async-done(((bf16[512,1024]{1,0:T(8,128)(2,1)}), bf16[1024,1024]{1,0:T(8,128)(2,1)}) %all-gather.70.cloned.1.call-update) | async-done | bytes 2097168 | tf_op jit(solution)/shard_map/all_gather | solution.py:76
  139.8 49.9 %all-gather.74.cloned.1.call-done = bf16[512,3072]{1,0:T(8,128)(2,1)} async-done(((bf16[256,3072]{1,0:T(8,128)(2,1)}), bf16[512,3072]{1,0:T(8,128)(2,1)}) %all-gather.74.cloned.1.call-update) | async-done | bytes 3145744 | tf_op jit(solution)/shard_map/all_gather | solution.py:76
  190.3 49.3 %all-gather.78.cloned.1.call-done = bf16[512,3072]{1,0:T(8,128)(2,1)} async-done(((bf16[256,3072]{1,0:T(8,128)(2,1)}), bf16[512,3072]{1,0:T(8,128)(2,1)}) %all-gather.78.cloned.1.call-update) | async-done | bytes 3145744 | tf_op jit(solution)/shard_map/all_gather | solution.py:76
  239.9 16.1 %all-gather.64.cloned.1.call-done = bf16[2,512,1024]{2,1,0:T(8,128)(2,1)} async-done(((bf16[2,256,1024]{2,1,0:T(8,128)(2,1)}), bf16[2,512,1024]{2,1,0:T(8,128)(2,1)}) %all-gather.64.cloned.1.call-update) | async-done | bytes 2097168 | tf_op jit(solution)/shard_map/all_gather | solution.py:77
  256.0 2.9 copy.100
  261.1 11.2 all-gather.68.cloned.1.call-done
  278.2 13.5 %all-gather.60.cloned.1.call-done = bf16[2,512,2048]{2,1,0:T(8,128)(2,1)} async-done(((bf16[2,256,2048]{2,1,0:T(8,128)(2,1)}), bf16[2,512,2048]{2,1,0:T(8,128)(2,1)}) %all-gather.60.cloned.1.call-update) | async-done | bytes 4194320 | tf_op jit(solution)/shard_map/all_gather | solution.py:77
  291.7 6.4 copy.99
  298.1 3.5 multiply_reduce_fusion.3
  305.8 3.5 pad_maximum_fusion
  309.3 9.6 all-to-all-start
  319.2 56.7 %all-gather.82.cloned.1.call-done = bf16[1536,1024]{1,0:T(8,128)(2,1)} async-done(((bf16[768,1024]{1,0:T(8,128)(2,1)}), bf16[1536,1024]{1,0:T(8,128)(2,1)}) %all-gather.82.cloned.1.call-update) | async-done | bytes 3145744 | tf_op jit(solution)/shard_map/all_gather | solution.py:76
  378.1 14.4 %fusion.49 = (f32[2048]{0:T(1024)S(1)}, f32[2048,4096]{1,0:T(8,128)}) fusion(s32[2048]{0:T(1024)S(1)} %dynamic_slice.18, s32[4096]{0:T(1024)S(1)} %add.144, bf16[2048,128]{1,0:T(8,128)(2,1)S(1)} %bitcast.315, bf16[4096,128]{1,0:T(8,128)(2,1)S(1)} %bitcast.309), kind=kOutput, calls=%fused_computation.148 | convolution fusion | flops 2181036032 | bytes 35160064 | tf_op jit(solution)/shard_map/qd,kd->qk/dot_general | solution.py:200
  392.5 16.1 %exponential_reduce_fusion = f32[2048]{0:T(1024)S(1)} fusion(f32[2048]{0:T(1024)S(1)} %get-tuple-element.56, f32[2048,4096]{1,0:T(8,128)} %get-tuple-element.57, s32[2048]{0:T(1024)S(1)} %dynamic_slice.18, s32[4096]{0:T(1024)S(1)} %add.144), kind=kLoop, calls=%fused_computation.6 | loop fusion | flops 41940992 | bytes 33595392 | tf_op jit(solution)/shard_map/reduce_sum | solution.py:207
  408.6 18.5 %fusion.51 = (bf16[2048,128]{1,0:T(8,128)(2,1)S(1)}, f32[2048,128]{1,0:T(8,128)}) fusion(bf16[4096,128]{1,0:T(8,128)(2,1)S(1)} %bitcast.311, f32[2048]{0:T(1024)S(1)} %log_add_fusion, f32[2048,4096]{1,0:T(8,128)} %get-tuple-element.57, s32[2048]{0:T(1024)S(1)} %dynamic_slice.18, s32[4096]{0:T(1024)S(1)} %add.144), kind=kOutput, calls=%fused_computation.150 | convolution fusion | flops 2189688832 | bytes 36208640 | tf_op jit(solution)/shard_map/dot_general | solution.py:209
  427.5 29.0 %all_to_all.93 = bf16[32,128,128]{1,2,0:T(8,128)(2,1)S(1)} all-to-all(bf16[32,128,128]{1,2,0:T(8,128)(2,1)S(1)} %bitcast_select_fusion.3), channel_id=1, replica_groups=mesh['yh'=2,'x'=4,'z'=4,'yl'=2,'c'=2] {'yh','x','z'}, dimensions={0} | all-to-all | bytes 2097152 | tf_op jit(solution)/shard_map/all_to_all | solution.py:158
  456.5 3.7 multiply_reduce_fusion.8
  460.4 6.0 fusion.52
  466.4 5.0 fusion.53
  471.4 7.5 multiply_convert_fusion.1
  478.9 6.0 fusion.54
  484.9 5.6 multiply_reduce_fusion.5
  497.6 5.5 all-to-all-start.2
  503.5 20.3 %fusion.2 = bf16[4096,2048]{0,1:T(8,128)(2,1)} fusion(f32[2048,4096]{1,0:T(8,128)} %get-tuple-element.57, f32[2048]{0:T(1024)S(1)} %log_add_fusion, s32[4096]{0:T(1024)S(1)} %add.144, s32[2048]{0:T(1024)S(1)} %dynamic_slice.18), kind=kLoop, calls=%fused_computation.3 | loop fusion | flops 41943040 | bytes 50364416 | tf_op jit(solution)/shard_map/convert_element_type | solution.py:208
  523.8 22.5 %copy.101 = bf16[4096,2048]{1,0:T(8,128)(2,1)} copy(bf16[4096,2048]{0,1:T(8,128)(2,1)} %fusion.2) | data formatting | bytes 33554432 | tf_op jit(solution)/shard_map/dot_general | solution.py:64
  551.2 20.5 %multiply_convert_fusion = bf16[2048,4096]{1,0:T(8,128)(2,1)} fusion(f32[2048]{0:T(1024)S(1)} %multiply_reduce_fusion.2, f32[2048]{0:T(1024)S(1)} %log_add_fusion, bf16[2048,128]{1,0:T(8,128)(2,1)S(1)} %bitcast.266, bf16[4096,128]{1,0:T(8,128)(2,1)} %bitcast.312, f32[2048,4096]{1,0:T(8,128)} %get-tuple-element.57, s32[2048]{0:T(1024)S(1)} %dynamic_slice.18, ...), kind=kOutput, calls=%fused_computation.4 | convolution fusion | flops 2206203904 | bytes 51945472 | tf_op jit(solution)/shard_map/dot_general | solution.py:70
  571.7 9.3 fusion.8
  582.6 5.8 fusion.7
  594.9 10.3 convolution_convert_fusion.6
  605.2 3.2 pad_maximum_fusion.1
  608.4 9.3 all-to-all-start.3
  618.3 44.4 %all_gather.218 = bf16[2,128,1024]{2,1,0:T(8,128)(2,1)} all-gather(bf16[1,128,1024]{2,1,0:T(8,128)(2,1)S(1)} %copy-done.15), channel_id=1, replica_groups=mesh['yh'=2,'x'=4,'z'=4,'yl'=2,'c'=2] {'yl'}, dimensions={0}, use_global_device_ids=true | all-gather | bytes 786432 | tf_op jit(solution)/shard_map/all_gather | solution.py:76
  668.0 10.4 all-gather.17
  683.1 6.5 all_gather.200
  691.7 9.3 all-to-all-start.7
  702.2 22.4 %all_gather.203 = bf16[2,128,1024]{2,1,0:T(8,128)(2,1)} all-gather(bf16[1,128,1024]{2,1,0:T(8,128)(2,1)S(1)} %copy.94), channel_id=1, replica_groups=mesh['yh'=2,'x'=4,'z'=4,'yl'=2,'c'=2] {'yl'}, dimensions={0}, use_global_device_ids=true | all-gather | bytes 786432 | tf_op jit(solution)/shard_map/all_gather | solution.py:76
  725.8 6.1 all-to-all-start.5
  735.4 2.5 fusion.12
  740.0 4.2 all-to-all-start.6
  744.2 2.8 all-gather.92.cloned.1.call-done
  754.6 9.4 all-reduce.5
  764.4 5.7 all-to-all-start.4
  770.0 2.9 fusion.10
  774.4 8.2 all-gather.100.cloned.1.call-done
  782.6 2.9 fusion.11
  787.0 10.4 all-gather.88.cloned.1.call-done
  800.0 12.2 all-gather.90.cloned.1.call-done
  815.0 13.3 %all-gather.86.cloned.1.call-done = bf16[2,256,2048]{2,1,0:T(8,128)(2,1)} async-done(((bf16[2,128,2048]{2,1,0:T(8,128)(2,1)}), bf16[2,256,2048]{2,1,0:T(8,128)(2,1)}) %all-gather.86.cloned.1.call-update) | async-done | bytes 2097168 | tf_op jit(solution)/shard_map/all_gather | solution.py:77
  831.9 104.4 %concatenate.38 = bf16[3932736]{0:T(1024)(128)(2,1)} concatenate(bf16[524288]{0:T(1024)(128)(2,1)} %bitcast.273, bf16[262144]{0:T(1024)(128)(2,1)} %bitcast.293, bf16[262144]{0:T(1024)(128)(2,1)} %bitcast.294, bf16[524288]{0:T(1024)(128)(2,1)S(1)} %bitcast.272, bf16[786432]{0:T(1024)(128)(2,1)} %bitcast.262, bf16[786432]{0:T(1024)(128)(2,1)} %bitcast.263, ...), dimensions={0} | concatenate | bytes 15730944 | tf_op jit(solution)/shard_map/concatenate | solution.py:82
  936.3 8.3 pad_bitcast_fusion
  944.7 78.1 %reduce-scatter.3.cloned.1.call-done = bf16[7744,128]{1,0:T(8,128)(2,1)} async-done(((bf16[30976,128]{1,0:T(8,128)(2,1)}), bf16[7744,128]{1,0:T(8,128)(2,1)}) %reduce-scatter.3.cloned.1.call-update) | async-done | bytes 1982480 | tf_op jit(solution)/shard_map/reduce_scatter | solution.py:87
  1022.8 30.6 %reduce-scatter.5.cloned.1.call-done = bf16[1936,128]{1,0:T(8,128)(2,1)} async-done(((bf16[7744,128]{1,0:T(8,128)(2,1)}), bf16[1936,128]{1,0:T(8,128)(2,1)}) %reduce-scatter.5.cloned.1.call-update) | async-done | bytes 495632 | tf_op jit(solution)/shard_map/reduce_scatter | solution.py:88
  1053.4 14.6 %all-gather.24 = bf16[3872,128]{1,0:T(8,128)(2,1)S(1)} all-gather(bf16[1936,128]{1,0:T(8,128)(2,1)} %reduce-scatter.5.cloned.1.call-done), channel_id=26, replica_groups=mesh['yh'=2,'x'=4,'z'=4,'yl'=2,'c'=2] {'yh'}, dimensions={0}, use_global_device_ids=true | all-gather | bytes 1486848 | tf_op jit(solution)/shard_map/all_gather | solution.py:89
  1069.4 30.3 %all-gather.54.cloned.1.call-done = bf16[7744,128]{1,0:T(8,128)(2,1)} async-done(((bf16[1936,128]{1,0:T(8,128)(2,1)}), bf16[7744,128]{1,0:T(8,128)(2,1)}) %all-gather.54.cloned.1.call-update) | async-done | bytes 1982480 | tf_op jit(solution)/shard_map/all_gather | solution.py:91
  1099.8 4.6 fusion.21
  1105.5 75.5 %all-gather.56.cloned.1.call-done = bf16[30976,128]{1,0:T(8,128)(2,1)} async-done(((bf16[7744,128]{1,0:T(8,128)(2,1)}), bf16[30976,128]{1,0:T(8,128)(2,1)}) %all-gather.56.cloned.1.call-update) | async-done | bytes 7929872 | tf_op jit(solution)/shard_map/all_gather | solution.py:92
  1181.0 5.7 slice_convert_fusion
  1186.7 4.5 reshape.471
  1191.2 4.5 reshape.472
  1197.9 3.1 slice_convert_fusion.3
  1201.1 2.7 reshape.467
  (254 shorter events, 92.7 us)
Async XLA Ops:
  7.2 29.6 %all-gather.62.cloned.1.call-start = ((), (), s32[]{:S(2)}) async-start(), calls=%async_computation.17 | async-start | bytes 1572864 | tf_op jit(solution)/shard_map/all_gather | solution.py:76
  7.9 55.3 %all-gather.66.cloned.1.call-start = ((), (), s32[]{:S(2)}) async-start(), calls=%async_computation.19 | async-start | bytes 1572864 | tf_op jit(solution)/shard_map/all_gather | solution.py:76
  8.7 92.9 %all-gather.58.cloned.1.call-start = ((), (), s32[]{:S(2)}) async-start(), calls=%async_computation.15 | async-start | bytes 3145728 | tf_op jit(solution)/shard_map/all_gather | solution.py:76
  9.4 130.3 %all-gather.70.cloned.1.call-start = ((), (), s32[]{:S(2)}) async-start(), calls=%async_computation.21 | async-start | bytes 3145728 | tf_op jit(solution)/shard_map/all_gather | solution.py:76
  10.0 179.7 %all-gather.74.cloned.1.call-start = ((), (), s32[]{:S(2)}) async-start(), calls=%async_computation.23 | async-start | bytes 4718592 | tf_op jit(solution)/shard_map/all_gather | solution.py:76
  10.6 229.1 %all-gather.78.cloned.1.call-start = ((), (), s32[]{:S(2)}) async-start(), calls=%async_computation.25 | async-start | bytes 4718592 | tf_op jit(solution)/shard_map/all_gather | solution.py:76
  11.1 244.9 %all-gather.64.cloned.1.call-start = ((), (), s32[]{:S(2)}) async-start(), calls=%async_computation.18 | async-start | bytes 3145728 | tf_op jit(solution)/shard_map/all_gather | solution.py:77
  36.8 235.6 %all-gather.68.cloned.1.call-start = ((), (), s32[]{:S(2)}) async-start(), calls=%async_computation.20 | async-start | bytes 3145728 | tf_op jit(solution)/shard_map/all_gather | solution.py:77
  63.3 228.5 %all-gather.60.cloned.1.call-start = ((), (), s32[]{:S(2)}) async-start(), calls=%async_computation.16 | async-start | bytes 6291456 | tf_op jit(solution)/shard_map/all_gather | solution.py:77
  101.5 88.4 %copy-start.37 = (s32[1,64]{1,0:T(1,128)S(1)}, s32[1,64]{1,0:T(1,128)}, u32[]{:S(2)}) copy-start(s32[1,64]{1,0:T(1,128)} %param.16) | copy-start | bytes 772
  101.5 88.7 %copy-start = (bf16[1,128,1024]{2,1,0:T(8,128)(2,1)S(1)}, bf16[1,128,1024]{2,1,0:T(8,128)(2,1)}, u32[]{:S(2)}) copy-start(bf16[1,128,1024]{2,1,0:T(8,128)(2,1)} %param.14) | copy-start | bytes 786436
  101.6 274.3 %all-gather.82.cloned.1.call-start = ((), (), s32[]{:S(2)}) async-start(), calls=%async_computation.27 | async-start | bytes 4718592 | tf_op jit(solution)/shard_map/all_gather | solution.py:76
  102.2 354.4 %all-gather.72.cloned.1.call-start = ((), (), s32[]{:S(2)}) async-start(), calls=%async_computation.22 | async-start | bytes 6291456 | tf_op jit(solution)/shard_map/all_gather | solution.py:77
  139.7 320.7 %all-gather.76.cloned.1.call-start = ((), (), s32[]{:S(2)}) async-start(), calls=%async_computation.24 | async-start | bytes 9437184 | tf_op jit(solution)/shard_map/all_gather | solution.py:77
  189.7 69.2 %copy-start.27 = (f32[1024]{0:T(1024)S(1)}, f32[1024]{0:T(1024)}, u32[]{:S(2)}) copy-start(f32[1024]{0:T(1024)} %param.24) | copy-start | bytes 12292
  189.7 276.7 %all-gather.80.cloned.1.call-start = ((), (), s32[]{:S(2)}) async-start(), calls=%async_computation.26 | async-start | bytes 9437184 | tf_op jit(solution)/shard_map/all_gather | solution.py:77
  239.7 20.8 %copy-start.34 = (f32[128]{0:T(128)S(1)}, f32[128]{0:T(128)}, u32[]{:S(2)}) copy-start(f32[128]{0:T(128)} %param.27) | copy-start | bytes 1540
  239.7 58.4 %copy-start.32 = (f32[128]{0:T(128)}, f32[128]{0:T(128)S(1)}, u32[]{:S(2)}) copy-start(f32[128]{0:T(128)S(1)} %add_rsqrt_fusion.3) | copy-start | bytes 1540
  259.7 15.7 %copy-start.30 = (f32[128,8]{0,1:T(8,128)}, f32[128,8]{0,1:T(8,128)S(1)}, u32[]{:S(2)}) copy-start(f32[128,8]{0,1:T(8,128)S(1)} %add_rsqrt_fusion.1) | copy-start | bytes 12292
  309.3 66.6 %all-to-all-start = ((bf16[32,128,384]{2,1,0:T(8,128)(2,1)}), bf16[32,128,384]{2,1,0:T(8,128)(2,1)}, u32[]{:S(2)}, u32[]{:S(2)}) async-start(bf16[32,128,384]{2,1,0:T(8,128)(2,1)} %pad_maximum_fusion), calls=%async_computation | async-start | bytes 6291456 | tf_op jit(solution)/shard_map/all_to_all | solution.py:158
  318.9 152.4 %all-gather.84.cloned.1.call-start = ((), (), s32[]{:S(2)}) async-start(), calls=%async_computation.28 | async-start | bytes 9437184 | tf_op jit(solution)/shard_map/all_gather | solution.py:77
  378.0 14.5 %copy-start.22 = (bf16[32,128,128]{2,1,0:T(8,128)(2,1)}, bf16[32,128,128]{2,1,0:T(8,128)(2,1)S(1)}, u32[]{:S(2)}) copy-start(bf16[32,128,128]{2,1,0:T(8,128)(2,1)S(1)} %get-tuple-element.39) | copy-start | bytes 3145732
  378.0 30.5 %copy-start.24 = (bf16[32,128,128]{2,1,0:T(8,128)(2,1)}, bf16[32,128,128]{2,1,0:T(8,128)(2,1)S(1)}, u32[]{:S(2)}) copy-start(bf16[32,128,128]{2,1,0:T(8,128)(2,1)S(1)} %get-tuple-element.40) | copy-start | bytes 3145732
  378.1 14.4 %copy-start.25 = (bf16[16,128,128]{2,1,0:T(8,128)(2,1)}, bf16[16,128,128]{2,1,0:T(8,128)(2,1)S(1)}, u32[]{:S(2)}) copy-start(bf16[16,128,128]{2,1,0:T(8,128)(2,1)S(1)} %constant_dynamic-slice_fusion.2) | copy-start | bytes 1572868
  427.5 32.8 %copy-start.29 = (f32[1024]{0:T(1024)S(1)}, f32[1024]{0:T(1024)}, u32[]{:S(2)}) copy-start(f32[1024]{0:T(1024)} %param.25) | copy-start | bytes 12292
  466.4 5.0 copy-start.15
  484.9 5.8 copy-start.2
  490.5 4.9 copy-start.9
  497.6 48.8 %all-to-all-start.2 = ((bf16[32,128,128]{1,2,0:T(8,128)(2,1)}), bf16[32,128,128]{1,2,0:T(8,128)(2,1)}, u32[]{:S(2)}, u32[]{:S(2)}) async-start(bf16[32,128,128]{1,2,0:T(8,128)(2,1)} %bitcast_select_fusion.2), calls=%async_computation.2 | async-start | bytes 2097152 | tf_op jit(solution)/shard_map/all_to_all | solution.py:158
  503.1 175.4 %all-gather.94.cloned.1.call-start = ((), (), s32[]{:S(2)}) async-start(), calls=%async_computation.33 | async-start | bytes 2359296 | tf_op jit(solution)/shard_map/all_gather | solution.py:76
  551.2 20.5 %copy-start.23 = (bf16[32,128,128]{2,1,0:T(8,128)(2,1)S(1)}, bf16[32,128,128]{2,1,0:T(8,128)(2,1)}, u32[]{:S(2)}) copy-start(bf16[32,128,128]{2,1,0:T(8,128)(2,1)} %copy-done.22) | copy-start | bytes 3145732
  571.7 9.3 copy-start.26
  571.7 10.9 copy-start.39
  608.4 54.4 %all-to-all-start.3 = ((bf16[32,128,384]{1,2,0:T(8,128)(2,1)}), bf16[32,128,384]{1,2,0:T(8,128)(2,1)}, u32[]{:S(2)}, u32[]{:S(2)}) async-start(bf16[32,128,384]{1,2,0:T(8,128)(2,1)} %pad_maximum_fusion.1), calls=%async_computation.3 | async-start | bytes 6291456 | tf_op jit(solution)/shard_map/all_to_all | solution.py:158
  617.7 61.4 %all-gather.98.cloned.1.call-start = ((), (), s32[]{:S(2)}) async-start(), calls=%async_computation.35 | async-start | bytes 2359296 | tf_op jit(solution)/shard_map/all_gather | solution.py:76
  618.3 117.1 %all-gather.102.cloned.1.call-start = ((), (), s32[]{:S(2)}) async-start(), calls=%async_computation.37 | async-start | bytes 1572864 | tf_op jit(solution)/shard_map/all_gather | solution.py:77
  662.8 76.7 %all-gather.52.cloned.1.call-start = ((), (), s32[]{:S(2)}) async-start(), calls=%async_computation.10 | async-start | bytes 1572864 | tf_op jit(solution)/shard_map/all_gather | solution.py:76
  667.9 79.1 %all-gather.92.cloned.1.call-start = ((), (), s32[]{:S(2)}) async-start(), calls=%async_computation.32 | async-start | bytes 1572864 | tf_op jit(solution)/shard_map/all_gather | solution.py:77
  678.4 91.6 %all-gather.96.cloned.1.call-start = ((), (), s32[]{:S(2)}) async-start(), calls=%async_computation.34 | async-start | bytes 4718592 | tf_op jit(solution)/shard_map/all_gather | solution.py:77
  679.0 103.6 %all-gather.100.cloned.1.call-start = ((), (), s32[]{:S(2)}) async-start(), calls=%async_computation.36 | async-start | bytes 4718592 | tf_op jit(solution)/shard_map/all_gather | solution.py:77
  679.8 117.6 %all-gather.88.cloned.1.call-start = ((), (), s32[]{:S(2)}) async-start(), calls=%async_computation.30 | async-start | bytes 1572864 | tf_op jit(solution)/shard_map/all_gather | solution.py:77
  682.9 41.9 %copy-start.28 = (f32[1024]{0:T(1024)S(1)}, f32[1024]{0:T(1024)}, u32[]{:S(2)}) copy-start(f32[1024]{0:T(1024)} %param.24) | copy-start | bytes 12292
  689.6 42.3 %copy-start.33 = (f32[128]{0:T(128)S(1)}, f32[128]{0:T(128)}, u32[]{:S(2)}) copy-start(f32[128]{0:T(128)} %copy-done.32) | copy-start | bytes 1540
  691.7 41.1 %copy-start.38 = (u32[128]{0:T(128)S(1)}, u32[128]{0:T(128)}, u32[]{:S(2)}) copy-start(u32[128]{0:T(128)} %constant.91) | copy-start | bytes 1540
  691.7 34.2 %all-to-all-start.7 = ((bf16[128,4,768]{2,0,1:T(8,128)(2,1)}), bf16[128,4,768]{2,0,1:T(8,128)(2,1)}, u32[]{:S(2)}, u32[]{:S(2)}) async-start(bf16[128,4,768]{2,0,1:T(8,128)(2,1)} %bitcast.240), calls=%async_computation.7 | async-start | bytes 1572864 | tf_op jit(solution)/shard_map/all_to_all | solution.py:296
  700.9 111.2 %all-gather.90.cloned.1.call-start = ((), (), s32[]{:S(2)}) async-start(), calls=%async_computation.31 | async-start | bytes 1572864 | tf_op jit(solution)/shard_map/all_gather | solution.py:77
  702.0 33.4 %copy-start.19 = (bf16[128,8,128]{0,2,1:T(8,128)(2,1)}, bf16[128,8,128]{0,2,1:T(8,128)(2,1)S(1)}, u32[]{:S(2)}) copy-start(bf16[128,8,128]{0,2,1:T(8,128)(2,1)S(1)} %slice.169) | copy-start | bytes 786436
  725.8 14.1 %all-to-all-start.5 = ((bf16[128,4,512]{2,0,1:T(8,128)(2,1)}), bf16[128,4,512]{2,0,1:T(8,128)(2,1)}, u32[]{:S(2)}, u32[]{:S(2)}) async-start(bf16[128,4,512]{2,0,1:T(8,128)(2,1)} %copy.95), calls=%async_computation.5 | async-start | bytes 1048576 | tf_op jit(solution)/shard_map/all_to_all | solution.py:294
  731.9 96.4 %all-gather.86.cloned.1.call-start = ((), (), s32[]{:S(2)}) async-start(), calls=%async_computation.29 | async-start | bytes 3145728 | tf_op jit(solution)/shard_map/all_gather | solution.py:77
  737.9 12.7 %copy-start.5 = (bf16[2,512,1024]{2,1,0:T(8,128)(2,1)S(1)}, bf16[2,512,1024]{2,1,0:T(8,128)(2,1)}, u32[]{:S(2)}) copy-start(bf16[2,512,1024]{2,1,0:T(8,128)(2,1)} %all-gather.64.cloned.1.call-done) | copy-start | bytes 6291460
  740.0 24.4 %all-to-all-start.6 = ((bf16[128,4,256]{2,0,1:T(8,128)(2,1)}), bf16[128,4,256]{2,0,1:T(8,128)(2,1)S(1)}, u32[]{:S(2)}, u32[]{:S(2)}) async-start(bf16[128,4,256]{2,0,1:T(8,128)(2,1)} %bitcast.308), calls=%async_computation.6 | async-start | bytes 524288 | tf_op jit(solution)/shard_map/all_to_all | solution.py:295
  747.0 4.4 copy-start.20
  764.4 22.6 %all-to-all-start.4 = ((bf16[128,4,256]{2,0,1:T(8,128)(2,1)}), bf16[128,4,256]{2,0,1:T(8,128)(2,1)S(1)}, u32[]{:S(2)}, u32[]{:S(2)}) async-start(bf16[128,4,256]{2,0,1:T(8,128)(2,1)} %fusion.24), calls=%async_computation.4 | async-start | bytes 524288 | tf_op jit(solution)/shard_map/all_to_all | solution.py:293
  770.0 252.7 %reduce-scatter.3.cloned.1.call-start = ((), (), s32[]{:S(2)}) async-start(), calls=%async_computation.11 | async-start | bytes 9912320 | tf_op jit(solution)/shard_map/reduce_scatter | solution.py:87
  787.0 25.2 %copy-start.12 = (bf16[128,4,256]{2,0,1:T(8,128)(2,1)}, bf16[128,4,256]{2,0,1:T(8,128)(2,1)S(1)}, u32[]{:S(2)}) copy-start(bf16[128,4,256]{2,0,1:T(8,128)(2,1)S(1)} %all-to-all-done.4) | copy-start | bytes 786436
  812.2 19.8 %copy-start.7 = (bf16[96,8,8,128]{3,1,2,0:T(8,128)(2,1)S(1)}, bf16[96,8,8,128]{3,1,2,0:T(8,128)(2,1)}, u32[]{:S(2)}) copy-start(bf16[96,8,8,128]{3,1,2,0:T(8,128)(2,1)} %copy.113) | copy-start | bytes 4718596
  812.2 19.8 %copy-start.11 = (bf16[64,8,8,128]{3,1,2,0:T(8,128)(2,1)S(1)}, bf16[64,8,8,128]{3,1,2,0:T(8,128)(2,1)}, u32[]{:S(2)}) copy-start(bf16[64,8,8,128]{3,1,2,0:T(8,128)(2,1)} %copy.110) | copy-start | bytes 3145732
  944.6 155.1 %copy-start.14 = (bf16[128,3072]{1,0:T(8,128)(2,1)S(1)}, bf16[128,3072]{1,0:T(8,128)(2,1)}, u32[]{:S(2)}) copy-start(bf16[128,3072]{1,0:T(8,128)(2,1)} %get-tuple-element.38) | copy-start | bytes 2359300
  944.6 108.8 %reduce-scatter.5.cloned.1.call-start = ((), (), s32[]{:S(2)}) async-start(), calls=%async_computation.12 | async-start | bytes 2478080 | tf_op jit(solution)/shard_map/reduce_scatter | solution.py:88
  1022.7 77.0 %all-gather.54.cloned.1.call-start = ((), (), s32[]{:S(2)}) async-start(), calls=%async_computation.13 | async-start | bytes 2478080 | tf_op jit(solution)/shard_map/all_gather | solution.py:91
  1069.1 111.9 %all-gather.56.cloned.1.call-start = ((), (), s32[]{:S(2)}) async-start(), calls=%async_computation.14 | async-start | bytes 9912320 | tf_op jit(solution)/shard_map/all_gather | solution.py:92
  1099.8 4.7 copy-start.10
  1099.8 4.7 copy-start.16
  1099.8 4.7 copy-start.21
  (11 other events, 27.7 us)
Sparse Core Ops, SparseCore 0:
  9.7 27.0 all-gather.61
  38.4 24.7 all-gather.65
  64.9 36.6 all-gather.57
  103.0 36.6 all-gather.69
  141.2 48.4 all-gather.73
  191.2 48.4 all-gather.77
  241.3 14.6 all-gather.63
  257.7 14.6 all-gather.67
  274.0 17.6 all-gather.59
  293.2 82.5 all-gather.81
  377.5 21.7 all-gather.71
  400.8 20.8 all-gather.75
  423.4 20.7 all-gather.79
  445.7 20.7 all-gather.83
  546.5 31.9 all-gather.93
  620.4 57.1 all-gather.97
  679.2 15.1 all-gather.101
  696.5 32.7 all-gather.51
  730.9 16.0 all-gather.91
  748.5 16.2 all-gather.95
  766.4 16.1 all-gather.99
  784.3 13.0 all-gather.87
  799.0 13.0 all-gather.89
  813.7 14.6 all-gather.85
  944.7 77.9 reduce-scatter.2
  1025.0 28.3 reduce-scatter.4
  1069.2 30.4 all-gather.53
  1101.5 79.5 all-gather.55
